TPU v7x, 32 devices: a whole 2x2x4 slice. The times are simulated.
32 devices in a mesh: groups: 2 (over y), req: 4 (over z), head: 2 (over x), pair: 2 (over core).
Axes of the slice: x: 2, y: 2, z: 4, core: 2. Of those that a mesh axis runs over, the one named last changes fastest.
Arguments:
- query: bfloat16 [256, 8192], P(('groups', 'req', 'pair'), 'head'), parts along dimension 0, may hold values from -80 to 80
- new_keys: bfloat16 [256, 512], P(('groups', 'req', 'pair'), 'head'), parts along dimension 0, may hold values from -4 to 4
- new_values: bfloat16 [256, 512], P(('groups', 'req', 'pair'), 'head'), parts along dimension 0, may hold values from -4 to 4
- key_cache: bfloat16 [256, 512, 512], P(('groups', 'req', 'pair'), None, 'head'), parts along dimension 0, may hold values from -4 to 4
- value_cache: bfloat16 [256, 512, 512], P(('groups', 'req', 'pair'), None, 'head'), parts along dimension 0, may hold values from -4 to 4
- lengths: int32 [256], P(('groups', 'req', 'pair')), parts along dimension 0, may hold values from 1 to 512, as said below
- residual: bfloat16 [256, 8192], P(('groups', 'req', 'pair'), 'head'), parts along dimension 0, may hold values from -1.6 to 1.6
- norm_gain: float32 [8192], P('head'), may hold values from 0.5 to 1.5
- gate_weight: bfloat16 [26624, 8192], P(('req', 'pair'), 'head'), may hold values from -0.0625 to 0.0625
- up_weight: bfloat16 [26624, 8192], P(('req', 'pair'), 'head'), may hold values from -0.0625 to 0.0625
- down_weight: bfloat16 [26624, 8192], P(('req', 'pair'), 'head'), may hold values from -0.0390625 to 0.0390625
Outputs:
- mixed: bfloat16 [256, 8192], P(('groups', 'req', 'pair'), 'head'), parts along dimension 0
There are 2 independent parts, one for each index of `groups`. A program takes and returns all parts, laid end to end along the dimension named above; an argument that names none is the same for every part. Nothing has to cross between parts.
Inputs may be any that keep to these rules, and one draw needn't show every extreme that they name: `lengths`: every row has at least one cached position in use; in every draw some row uses all 512.
All inputs are finite; a program needn't handle non-finite values.
Results may differ from a plain program's by a relative error of at most 0.023.
Values may be sent and summed in bfloat16 or wider, within the bound.
A program may use at most 192 MiB of HBM per device.

v0:
```python
import math

import jax
import jax.numpy as jnp
from jax import lax
from jax.sharding import PartitionSpec as P

HEAD_DIM = 128
GROUP = 16
D = 8192
CACHE = 512


highest = lax.Precision.HIGHEST
contract_last = (((1,), (1,)), ((), ()))
low_value = -1e30


def local(
    query,
    new_keys,
    new_values,
    key_cache,
    value_cache,
    lengths,
    residual,
    norm_gain,
    gate_weight,
    up_weight,
    down_weight,
):
    slot_rows = query.shape[0]
    local_kv = new_keys.shape[1] // HEAD_DIM
    score_scale = 1.0 / math.sqrt(HEAD_DIM)
    query_heads = query.reshape(slot_rows, local_kv, GROUP, HEAD_DIM)
    key_heads = key_cache.reshape(slot_rows, CACHE, local_kv, HEAD_DIM)
    scores = (
        jnp.einsum("sgjd,stgd->sgjt", query_heads, key_heads, preferred_element_type=jnp.float32)
        * score_scale
    )
    own_score = (
        jnp.einsum(
            "sgjd,sgd->sgj",
            query_heads,
            new_keys.reshape(slot_rows, local_kv, HEAD_DIM),
            preferred_element_type=jnp.float32,
        )
        * score_scale
    )
    is_live = lax.broadcasted_iota(jnp.int32, (slot_rows, CACHE), 1) < lengths[:, None]
    live_mask = is_live[:, None, None, :]
    row_max = jnp.maximum(jnp.max(jnp.where(live_mask, scores, low_value), axis=3), own_score)
    weights = jnp.where(live_mask, jnp.exp(scores - row_max[..., None]), 0.0)
    own_weight = jnp.exp(own_score - row_max)
    weight_sum = jnp.sum(weights, axis=3) + own_weight
    value_heads = value_cache.reshape(slot_rows, CACHE, local_kv, HEAD_DIM).astype(jnp.float32)
    summed = jnp.einsum("sgjt,stgd->sgjd", weights, value_heads, precision=highest)
    summed = summed + own_weight[..., None] * new_values.reshape(
        slot_rows, local_kv, 1, HEAD_DIM
    ).astype(jnp.float32)
    attention = (summed / weight_sum[..., None]).reshape(slot_rows, local_kv * GROUP * HEAD_DIM)
    stream = residual.astype(jnp.float32) + attention
    squares = lax.psum(jnp.sum(stream * stream, axis=1), "head")
    normed = (stream * lax.rsqrt(squares[:, None] / D + 1e-05) * norm_gain).astype(jnp.bfloat16)
    block_rows = lax.all_gather(normed, ("req", "pair"), axis=0, tiled=True)
    gate_out = lax.dot_general(
        block_rows, gate_weight, contract_last, preferred_element_type=jnp.float32
    )
    up_out = lax.dot_general(
        block_rows, up_weight, contract_last, preferred_element_type=jnp.float32
    )
    unit_parts = jnp.concatenate([gate_out, up_out], axis=1)
    unit_count = gate_weight.shape[0]
    unit_share = lax.psum_scatter(unit_parts, "head", scatter_dimension=0, tiled=True)
    hidden_share = (jax.nn.silu(unit_share[:, :unit_count]) * unit_share[:, unit_count:]).astype(
        jnp.bfloat16
    )
    hidden = lax.all_gather(hidden_share, "head", axis=0, tiled=True)
    ffn_out = lax.psum_scatter(
        jnp.dot(hidden, down_weight, preferred_element_type=jnp.float32).astype(jnp.bfloat16),
        ("req", "pair"),
        scatter_dimension=0,
        tiled=True,
    ).astype(jnp.float32)
    return (stream + ffn_out).astype(jnp.bfloat16)


def solution(mesh):
    return jax.shard_map(
        local,
        mesh=mesh,
        in_specs=(
            P(("groups", "req", "pair"), "head"),
            P(("groups", "req", "pair"), "head"),
            P(("groups", "req", "pair"), "head"),
            P(("groups", "req", "pair"), None, "head"),
            P(("groups", "req", "pair"), None, "head"),
            P(("groups", "req", "pair")),
            P(("groups", "req", "pair"), "head"),
            P("head"),
            P(("req", "pair"), "head"),
            P(("req", "pair"), "head"),
            P(("req", "pair"), "head"),
        ),
        out_specs=P(("groups", "req", "pair"), "head"),
        check_vma=False,
    )
```

profile of v0, /device:TPU:0, one launch (start us, length us, event | category | flops | bytes accessed | tf_op | source)
XLA Modules:
  0.0 198.7 jit_solution(4457470929542562215)
XLA Ops:
  6.5 0.0 all-gather.2.cloned.1.call-start
  6.5 0.7 iota_compare_fusion
  7.3 0.7 reshape.57
  8.0 0.7 reshape.53
  8.7 0.0 copy-start.3
  8.7 1.1 copy.18
  9.8 0.2 fusion.22
  9.9 3.5 %select_reduce_fusion = (f32[16,2,16]{2,1,0:T(2,128)S(1)}, f32[16,2,16,512]{3,2,1,0:T(8,128)S(1)}) fusion(pred[16,512]{1,0:T(8,128)(4,1)S(1)} %iota_compare_fusion, bf16[16,2,16,128]{3,2,1,0:T(8,128)(2,1)S(1)} %bitcast.50, bf16[16,512,256]{2,1,0:T(8,128)(2,1)} %param.14), kind=kOutput, calls=%fused_computation.12 | convolution fusion | flops 67894784 | bytes 5384192 | tf_op jit(solution)/shard_map/sgjd,stgd->sgjt/dot_general | solution.py:38
  13.5 0.0 copy-start.1
  13.5 0.0 copy-start.2
  13.5 0.4 fusion.15
  14.0 0.0 copy-done.3
  14.0 2.0 fusion.12
  16.0 0.3 multiply_reduce_fusion
  16.2 5.9 %psum.7 = f32[16]{0:T(128)S(1)} all-reduce(f32[16]{0:T(128)S(1)} %multiply_reduce_fusion), channel_id=1, replica_groups=mesh['groups'=2,'req'=4,'head'=2,'pair'=2] {'head'}, use_global_device_ids=true, to_apply=%region_3.4 | all-reduce | flops 16 | bytes 128 | tf_op jit(solution)/shard_map/psum | solution.py:63
  22.1 0.0 copy-done.2
  22.1 0.8 multiply_convert_fusion
  22.9 0.0 all-gather.2.cloned.1.call-update
  22.9 0.0 reduce-scatter.3.cloned.1.call-start
  23.0 24.1 %all-gather.2.cloned.1.call-done = bf16[128,4096]{1,0:T(8,128)(2,1)} async-done(((bf16[16,4096]{1,0:T(8,128)(2,1)}), bf16[128,4096]{1,0:T(8,128)(2,1)}) %all-gather.2.cloned.1.call-update) | async-done | bytes 1048592 | tf_op jit(solution)/shard_map/all_gather | solution.py:65
  47.1 18.0 %fusion.24 = f32[128,3328]{1,0:T(8,128)S(1)} fusion(bf16[128,4096]{1,0:T(8,128)(2,1)} %all-gather.2.cloned.1.call-done, bf16[3328,4096]{1,0:T(8,128)(2,1)} %param.20), kind=kOutput, calls=%fused_computation.31 | convolution fusion | flops 3489660928 | bytes 30015488 | tf_op jit(solution)/shard_map/dot_general | solution.py:69
  65.1 15.4 %fusion.23 = f32[128,3328]{1,0:T(8,128)} fusion(bf16[128,4096]{1,0:T(8,128)(2,1)S(1)} %copy-done, bf16[3328,4096]{1,0:T(8,128)(2,1)} %param.19), kind=kOutput, calls=%fused_computation.30 | convolution fusion | flops 3489660928 | bytes 30015488 | tf_op jit(solution)/shard_map/dot_general | solution.py:66
  80.5 3.5 %pad_maximum_fusion = f32[128,6656]{1,0:T(8,128)} fusion(f32[128,3328]{1,0:T(8,128)S(1)} %fusion.24, f32[128,3328]{1,0:T(8,128)} %fusion.23), kind=kLoop, calls=%fused_computation.7 | loop fusion | flops 851968 | bytes 6815744 | tf_op jit(solution)/shard_map/concatenate | solution.py:72
  84.0 0.0 reduce-scatter.3.cloned.1.call-update
  84.1 0.0 reduce-scatter.5.cloned.1.call-start
  84.1 46.0 %reduce-scatter.3.cloned.1.call-done = f32[64,6656]{1,0:T(8,128)} async-done(((f32[128,6656]{1,0:T(8,128)}), f32[64,6656]{1,0:T(8,128)}) %reduce-scatter.3.cloned.1.call-update) | async-done | bytes 1703952 | tf_op jit(solution)/shard_map/reduce_scatter | solution.py:74
  130.1 1.6 fusion.16
  131.8 12.2 %all_gather.7 = bf16[128,3328]{1,0:T(8,128)(2,1)S(1)} all-gather(bf16[64,3328]{1,0:T(8,128)(2,1)S(1)} %fusion.16), channel_id=1, replica_groups=mesh['groups'=2,'req'=4,'head'=2,'pair'=2] {'head'}, dimensions={0}, use_global_device_ids=true | all-gather | bytes 1277952 | tf_op jit(solution)/shard_map/all_gather | solution.py:78
  144.0 13.7 %convolution_convert_fusion = bf16[128,4096]{1,0:T(8,128)(2,1)} fusion(bf16[128,3328]{1,0:T(8,128)(2,1)S(1)} %all_gather.7, bf16[3328,4096]{1,0:T(8,128)(2,1)} %param.21), kind=kOutput, calls=%fused_computation | convolution fusion | flops 3490185216 | bytes 29163520 | tf_op jit(solution)/shard_map/dot_general | solution.py:80
  157.7 0.0 reduce-scatter.5.cloned.1.call-update
  157.8 32.7 %reduce-scatter.5.cloned.1.call-done = bf16[16,4096]{1,0:T(8,128)(2,1)} async-done(((bf16[128,4096]{1,0:T(8,128)(2,1)}), bf16[16,4096]{1,0:T(8,128)(2,1)}) %reduce-scatter.5.cloned.1.call-update) | async-done | bytes 131088 | tf_op jit(solution)/shard_map/reduce_scatter | solution.py:79
  190.5 1.7 add_convert_fusion
  (6 shorter events, 0.1 us)
Async XLA Ops:
  6.5 40.6 %all-gather.2.cloned.1.call-start = ((), (), s32[]{:S(2)}) async-start(), calls=%async_computation.2 | async-start | bytes 1179648 | tf_op jit(solution)/shard_map/all_gather | solution.py:65
  8.7 5.3 %copy-start.3 = (bf16[16,512,256]{2,1,0:T(8,128)(2,1)S(1)}, bf16[16,512,256]{2,1,0:T(8,128)(2,1)}, u32[]{:S(2)}) copy-start(bf16[16,512,256]{2,1,0:T(8,128)(2,1)} %param.15) | copy-start | bytes 12582916
  13.5 2.5 %copy-start.1 = (bf16[16,4096]{1,0:T(8,128)(2,1)S(1)}, bf16[16,4096]{1,0:T(8,128)(2,1)}, u32[]{:S(2)}) copy-start(bf16[16,4096]{1,0:T(8,128)(2,1)} %param.17) | copy-start | bytes 393220
  13.5 8.6 %copy-start.2 = (f32[4096]{0:T(1024)S(1)}, f32[4096]{0:T(1024)}, u32[]{:S(2)}) copy-start(f32[4096]{0:T(1024)} %param.18) | copy-start | bytes 49156
  22.9 107.2 %reduce-scatter.3.cloned.1.call-start = ((), (), s32[]{:S(2)}) async-start(), calls=%async_computation.3 | async-start | bytes 5111808 | tf_op jit(solution)/shard_map/reduce_scatter | solution.py:74
  47.1 18.0 %copy-start = (bf16[128,4096]{1,0:T(8,128)(2,1)S(1)}, bf16[128,4096]{1,0:T(8,128)(2,1)}, u32[]{:S(2)}) copy-start(bf16[128,4096]{1,0:T(8,128)(2,1)} %all-gather.2.cloned.1.call-done) | copy-start | bytes 3145732
  84.1 106.4 %reduce-scatter.5.cloned.1.call-start = ((), (), s32[]{:S(2)}) async-start(), calls=%async_computation.4 | async-start | bytes 1179648 | tf_op jit(solution)/shard_map/reduce_scatter | solution.py:79
Sparse Core Ops, SparseCore 0:
  23.1 24.0 all-gather.1
  84.2 45.8 reduce-scatter.2
  157.9 32.5 reduce-scatter.4
where the time goes:
time: 199 us
  waiting for transfers between devices  103 us (52%)
  matrix products  52.8 us (27%)
  blocking collectives  18.1 us (9%)
  between operations  13.2 us (7%)
  other arithmetic  9.15 us (5%)
  local copies, waits for them, and re-layouts  2.52 us (1%)
    reduce_scatter x1, waiting for transfers between devices, local(): lax.psum_scatter(unit_parts, 'head', scatter_dimension=0, tiled=True)  46 us
    reduce_scatter x1, waiting for transfers between devices, local(): lax.psum_scatter(jnp.dot(hidden, down_weight, preferred_element_type=jnp....  32.7 us
    all_gather x1, waiting for transfers between devices, local(): block_rows = lax.all_gather(normed, ('req', 'pair'), axis=0, tiled=True)  24.1 us
    dot_general x1, matrix products, local(): lax.dot_general(block_rows, up_weight, contract_last, preferred_element_t...  18 us
    dot_general x1, matrix products, local(): lax.dot_general(block_rows, gate_weight, contract_last, preferred_element...  15.4 us
    dot_general x1, matrix products, local(): jnp.dot(hidden, down_weight, preferred_element_type=jnp.float32)  13.7 us
    all_gather x1, blocking collectives, local(): hidden = lax.all_gather(hidden_share, 'head', axis=0, tiled=True)  12.2 us
    psum x1, blocking collectives, local(): squares = lax.psum(jnp.sum(stream * stream, axis=1), 'head')  5.86 us
  transfers between devices with their start and end apart: 3, of which 3 were waited for; matrix products, arithmetic and copies ran while one was open for 0% of the time, Pallas kernels for 0%

commit v1 on v0

--- a/solution.py
+++ b/solution.py
@@ -1,8 +1,11 @@
+import functools
 import math
 
 import jax
 import jax.numpy as jnp
 from jax import lax
+from jax.experimental import pallas as pl
+from jax.experimental.pallas import tpu as pltpu
 from jax.sharding import PartitionSpec as P
 
 HEAD_DIM = 128
@@ -16,7 +19,234 @@
 low_value = -1e30
 
 
+MESH = pl.DeviceIdType.MESH
+HIDDEN_LAG = 3
+DOWN_LAG = 6
+SLOT_BYTES = 40 * 2**20
+
+
+def block_kernel(
+    sizes,
+    stream_ref, gain_ref, gate_hbm, up_hbm, down_hbm, out_ref,
+    wbuf, ssum, xg, tf, pb, precv, hid, acc, psd, prv, zs, zr,
+    wsem, ss_send, ss_recv, ag_send, ag_recv, agp_send, agp_recv,
+    rs_send, rs_recv, hg_send, hg_recv, pr_send, pr_recv, z_send, z_recv,
+):
+    reqs, heads, chunks, unit, slots, rows, feats, total_feats = sizes
+    block = reqs * 2 * rows
+    part = block // heads
+    my_req = lax.axis_index("req")
+    my_head = lax.axis_index("head")
+    my_pair = lax.axis_index("pair")
+    other = 1 - my_pair
+    head_peers = [lax.rem(my_head + d, heads) for d in range(1, heads)]
+    req_peers = [lax.rem(my_req + d, reqs) for d in range(1, reqs)]
+    loads = 3 * chunks
+
+    def remote(src, dst, send, recv, device):
+        return pltpu.make_async_remote_copy(
+            src_ref=src, dst_ref=dst, send_sem=send, recv_sem=recv,
+            device_id=device, device_id_type=MESH,
+        )
+
+    def load_of(hbm, chunk, slot):
+        return pltpu.make_async_copy(
+            hbm.at[pl.ds(pl.multiple_of(chunk * unit, unit), unit)], wbuf.at[slot], wsem.at[slot]
+        )
+
+    for j in range(min(slots, loads)):
+        if j < 2 * chunks:
+            load_of(up_hbm if j % 2 else gate_hbm, j // 2, j).start()
+        else:
+            load_of(down_hbm, j - 2 * chunks, j).start()
+
+    barrier = pltpu.get_barrier_semaphore()
+    for peer in head_peers:
+        pl.semaphore_signal(barrier, inc=1, device_id={"head": peer}, device_id_type=MESH)
+    for peer in req_peers:
+        pl.semaphore_signal(barrier, inc=1, device_id={"req": peer}, device_id_type=MESH)
+    pl.semaphore_signal(barrier, inc=1, device_id={"pair": other}, device_id_type=MESH)
+    pl.semaphore_wait(barrier, heads + reqs - 1)
+
+    stream = stream_ref[...]
+    squares = jnp.sum(stream * stream, axis=1, keepdims=True)
+    ssum[my_head] = jnp.broadcast_to(squares, (rows, HEAD_DIM))
+
+    def square_copy(owner, peer):
+        return remote(ssum.at[owner], ssum.at[owner], ss_send.at[peer], ss_recv.at[owner], {"head": peer})
+
+    for peer in head_peers:
+        square_copy(my_head, peer).start()
+    for peer in head_peers:
+        square_copy(peer, peer).wait_recv()
+    mean = jnp.sum(ssum[...], axis=0)[:, :1] / total_feats
+    xg[my_req, my_pair] = (stream * lax.rsqrt(mean + 1e-05) * gain_ref[...]).astype(jnp.bfloat16)
+
+    def gather_copy(owner, peer):
+        here = xg.at[owner, my_pair]
+        return remote(here, here, ag_send.at[peer], ag_recv.at[owner], {"req": peer})
+
+    def pair_copy(owner, side):
+        here = xg.at[owner, side]
+        return remote(here, here, agp_send.at[owner], agp_recv.at[owner], {"pair": other})
+
+    for peer in reversed(req_peers):
+        gather_copy(my_req, peer).start()
+    pair_copy(my_req, my_pair).start()
+    for peer in req_peers:
+        gather_copy(peer, peer).wait_recv()
+        pair_copy(peer, my_pair).start()
+    for owner in [my_req] + req_peers:
+        pair_copy(owner, other).wait_recv()
+
+    acc[...] = jnp.zeros_like(acc)
+
+    def sum_copy(chunk, owner, peer):
+        return remote(
+            pb.at[chunk, peer], precv.at[chunk, owner],
+            rs_send.at[chunk, peer], rs_recv.at[chunk, owner], {"head": peer},
+        )
+
+    def hidden_copy(chunk, owner, peer):
+        here = hid.at[chunk, owner]
+        return remote(here, here, hg_send.at[chunk, peer], hg_recv.at[chunk, owner], {"head": peer})
+
+    def step(t, carry):
+        @pl.when(t < chunks)
+        def _():
+            for side, hbm in enumerate((gate_hbm, up_hbm)):
+                slot = lax.rem(2 * t + side, slots)
+                load_of(hbm, t, slot).wait()
+                x = xg[...].reshape(block, feats)
+                sums = lax.dot_general(
+                    x, wbuf[slot], contract_last, preferred_element_type=jnp.float32
+                ).reshape(heads, part, unit)
+                tf[t, :, side] = sums
+                pb[t, :, side] = sums.astype(jnp.bfloat16)
+            for peer in head_peers:
+                sum_copy(t, my_head, peer).start()
+            for side in range(2):
+                later = slots + 2 * t + side
+                slot = lax.rem(later, slots)
+
+                @pl.when(later < 2 * chunks)
+                def _():
+                    load_of((gate_hbm, up_hbm)[side], later // 2, slot).start()
+
+                @pl.when((later >= 2 * chunks) & (later < loads))
+                def _():
+                    load_of(down_hbm, later - 2 * chunks, slot).start()
+
+        @pl.when((t >= HIDDEN_LAG) & (t < chunks + HIDDEN_LAG))
+        def _():
+            k = t - HIDDEN_LAG
+            gate = tf[k, my_head, 0]
+            up = tf[k, my_head, 1]
+            for peer in head_peers:
+                sum_copy(k, peer, peer).wait_recv()
+                gate = gate + precv[k, peer, 0].astype(jnp.float32)
+                up = up + precv[k, peer, 1].astype(jnp.float32)
+            hid[k, my_head] = (jax.nn.silu(gate) * up).astype(jnp.bfloat16)
+            for peer in head_peers:
+                hidden_copy(k, my_head, peer).start()
+
+        @pl.when(t >= DOWN_LAG)
+        def _():
+            k = t - DOWN_LAG
+            slot = lax.rem(2 * chunks + k, slots)
+            load_of(down_hbm, k, slot).wait()
+            for peer in head_peers:
+                hidden_copy(k, peer, peer).wait_recv()
+            h = hid[k].reshape(block, unit)
+            tile = 512
+            for c in range(0, feats, tile):
+                d = jnp.dot(h, wbuf[slot, :, c : c + tile], preferred_element_type=jnp.float32)
+                acc[:, :, :, c : c + tile] += d.reshape(reqs, 2, rows, tile)
+            for peer in head_peers:
+                sum_copy(k, my_head, peer).wait_send()
+                hidden_copy(k, my_head, peer).wait_send()
+
+        return carry
+
+    lax.fori_loop(0, chunks + DOWN_LAG, step, 0)
+
+    def swap_copy(owner):
+        return remote(psd.at[owner], prv.at[owner], pr_send.at[owner], pr_recv.at[owner], {"pair": other})
+
+    def total_copy(owner, peer):
+        return remote(zs.at[peer], zr.at[owner], z_send.at[peer], z_recv.at[owner], {"req": peer})
+
+    order = list(reversed(req_peers)) + [my_req]
+    for owner in order:
+        psd[owner] = acc[owner, other].astype(jnp.bfloat16)
+        swap_copy(owner).start()
+    for peer in order[:-1]:
+        swap_copy(peer).wait_recv()
+        zs[peer] = (acc[peer, my_pair] + prv[peer].astype(jnp.float32)).astype(jnp.bfloat16)
+        total_copy(my_req, peer).start()
+    swap_copy(my_req).wait_recv()
+    result = stream_ref[...] + acc[my_req, my_pair] + prv[my_req].astype(jnp.float32)
+    for peer in req_peers:
+        total_copy(peer, peer).wait_recv()
+        result = result + zr[peer].astype(jnp.float32)
+    out_ref[...] = result.astype(jnp.bfloat16)
+
+    for peer in head_peers:
+        square_copy(my_head, peer).wait_send()
+    for peer in req_peers:
+        gather_copy(my_req, peer).wait_send()
+        total_copy(my_req, peer).wait_send()
+    for owner in order:
+        pair_copy(owner, my_pair).wait_send()
+        swap_copy(owner).wait_send()
+
+
+def feed_forward(reqs, heads, stream, norm_gain, gate_weight, up_weight, down_weight):
+    rows, feats = stream.shape
+    units = gate_weight.shape[0]
+    unit = max(u for u in range(16, 257, 16) if units % u == 0)
+    chunks = units // unit
+    slots = min(3 * chunks, SLOT_BYTES // (unit * feats * 2) // 2 * 2)
+    block = reqs * 2 * rows
+    part = block // heads
+    sizes = (reqs, heads, chunks, unit, slots, rows, feats, D)
+    bf16, f32 = jnp.bfloat16, jnp.float32
+    dma = pltpu.SemaphoreType.DMA
+    vmem = pl.BlockSpec(memory_space=pltpu.VMEM)
+    hbm = pl.BlockSpec(memory_space=pl.ANY)
+    return pl.pallas_call(
+        functools.partial(block_kernel, sizes),
+        out_shape=jax.ShapeDtypeStruct((rows, feats), bf16),
+        in_specs=[vmem, vmem, hbm, hbm, hbm],
+        out_specs=vmem,
+        scratch_shapes=[
+            pltpu.VMEM((slots, unit, feats), bf16),
+            pltpu.VMEM((heads, rows, HEAD_DIM), f32),
+            pltpu.VMEM((reqs, 2, rows, feats), bf16),
+            pltpu.VMEM((chunks, heads, 2, part, unit), f32),
+            pltpu.VMEM((chunks, heads, 2, part, unit), bf16),
+            pltpu.VMEM((chunks, heads, 2, part, unit), bf16),
+            pltpu.VMEM((chunks, heads, part, unit), bf16),
+            pltpu.VMEM((reqs, 2, rows, feats), f32),
+            pltpu.VMEM((reqs, rows, feats), bf16),
+            pltpu.VMEM((reqs, rows, feats), bf16),
+            pltpu.VMEM((reqs, rows, feats), bf16),
+            pltpu.VMEM((reqs, rows, feats), bf16),
+            dma((slots,)),
+            dma((heads,)), dma((heads,)),
+            dma((reqs,)), dma((reqs,)), dma((reqs,)), dma((reqs,)),
+            dma((chunks, heads)), dma((chunks, heads)), dma((chunks, heads)), dma((chunks, heads)),
+            dma((reqs,)), dma((reqs,)), dma((reqs,)), dma((reqs,)),
+        ],
+        compiler_params=pltpu.CompilerParams(
+            collective_id=0, has_side_effects=True, vmem_limit_bytes=66_000_000
+        ),
+    )(stream, norm_gain.reshape(1, feats), gate_weight, up_weight, down_weight)
+
+
 def local(
+    reqs,
+    heads,
     query,
     new_keys,
     new_values,
@@ -60,34 +290,12 @@
     ).astype(jnp.float32)
     attention = (summed / weight_sum[..., None]).reshape(slot_rows, local_kv * GROUP * HEAD_DIM)
     stream = residual.astype(jnp.float32) + attention
-    squares = lax.psum(jnp.sum(stream * stream, axis=1), "head")
-    normed = (stream * lax.rsqrt(squares[:, None] / D + 1e-05) * norm_gain).astype(jnp.bfloat16)
-    block_rows = lax.all_gather(normed, ("req", "pair"), axis=0, tiled=True)
-    gate_out = lax.dot_general(
-        block_rows, gate_weight, contract_last, preferred_element_type=jnp.float32
-    )
-    up_out = lax.dot_general(
-        block_rows, up_weight, contract_last, preferred_element_type=jnp.float32
-    )
-    unit_parts = jnp.concatenate([gate_out, up_out], axis=1)
-    unit_count = gate_weight.shape[0]
-    unit_share = lax.psum_scatter(unit_parts, "head", scatter_dimension=0, tiled=True)
-    hidden_share = (jax.nn.silu(unit_share[:, :unit_count]) * unit_share[:, unit_count:]).astype(
-        jnp.bfloat16
-    )
-    hidden = lax.all_gather(hidden_share, "head", axis=0, tiled=True)
-    ffn_out = lax.psum_scatter(
-        jnp.dot(hidden, down_weight, preferred_element_type=jnp.float32).astype(jnp.bfloat16),
-        ("req", "pair"),
-        scatter_dimension=0,
-        tiled=True,
-    ).astype(jnp.float32)
-    return (stream + ffn_out).astype(jnp.bfloat16)
+    return feed_forward(reqs, heads, stream, norm_gain, gate_weight, up_weight, down_weight)
 
 
 def solution(mesh):
     return jax.shard_map(
-        local,
+        functools.partial(local, mesh.shape["req"], mesh.shape["head"]),
         mesh=mesh,
         in_specs=(
             P(("groups", "req", "pair"), "head"),

time: 199 us -> 93.1 us (0.47)
  waiting for transfers between devices: 103 us -> 0 us
  Pallas kernels: 0 us -> 81.1 us
  matrix products: 52.8 us -> 5.65 us
  blocking collectives: 18.1 us -> 0 us
  between operations: 13.2 us -> 0.07 us
  other arithmetic: 9.15 us -> 2.01 us
    pallas_call x0 -> x1, Pallas kernels: none -> 81.1 us  [feed_forward(): pl.pallas_call(functools.partial(block_kernel, sizes), out_shape=jax.Shap...]
    reduce_scatter x2 -> x0, waiting for transfers between devices: 78.8 us -> none  [the longest x1 46 us: local(): lax.psum_scatter(unit_parts, 'head', scatter_dimension=0, tiled=True)]
    dot_general x3 -> x0, matrix products: 47.1 us -> none  [the longest x1 18 us: local(): lax.dot_general(block_rows, up_weight, contract_last, preferred_element_t...]
    all_gather x1 -> x0, waiting for transfers between devices: 24.1 us -> none  [local(): block_rows = lax.all_gather(normed, ('req', 'pair'), axis=0, tiled=True)]
    all_gather x1 -> x0, blocking collectives: 12.2 us -> none  [local(): hidden = lax.all_gather(hidden_share, 'head', axis=0, tiled=True)]
    psum x1 -> x0, blocking collectives: 5.86 us -> none  [local(): squares = lax.psum(jnp.sum(stream * stream, axis=1), 'head')]
    convert_element_type x3 -> x0, other arithmetic: 4.19 us -> none  [the longest x1 1.72 us: local(): return (stream + ffn_out).astype(jnp.bfloat16)]
    concatenate x1 -> x0, other arithmetic: 3.53 us -> none  [local(): unit_parts = jnp.concatenate([gate_out, up_out], axis=1)]
  transfers between devices with their start and end apart: 3 -> 0, of which waited for: 3 -> 0; matrix products, arithmetic and copies ran while one was open for 0% -> 0% of each run, Pallas kernels for 0% -> 0%
where the time goes in v1:
time: 93.1 us; the launch traced here: 92.9 us
  Pallas kernels  81.1 us (87%)
  matrix products  5.65 us (6%)
  local copies, waits for them, and re-layouts  4.08 us (4%)
  other arithmetic  2.01 us (2%)
    pallas_call x1, Pallas kernels, feed_forward(): pl.pallas_call(functools.partial(block_kernel, sizes), out_shape=jax.Shap...  81.1 us
    dot_general x1, matrix products, local(): jnp.einsum('sgjd,stgd->sgjt', query_heads, key_heads, preferred_element_t...  3.52 us
    unnamed x6, local copies, waits for them, and re-layouts  2.67 us
    dot_general x1, matrix products, local(): jnp.einsum('sgjt,stgd->sgjd', weights, value_heads, precision=highest)  1.95 us

profile of v1, /device:TPU:0, one launch (start us, length us, event | category | flops | bytes accessed | tf_op | source)
XLA Modules:
  0.0 92.9 jit_solution(14120690563627914395)
XLA Ops:
  0.0 0.7 iota_compare_fusion
  0.7 0.7 reshape.56
  1.4 0.7 reshape.52
  2.1 0.0 copy-start.1
  2.2 1.1 %copy.18 = bf16[2,8,32,128]{3,2,1,0:T(8,128)(2,1)S(1)} copy(bf16[2,8,32,128]{3,1,2,0:T(8,128)(2,1)} %bitcast.38) | data formatting | bytes 262144
  3.2 0.2 fusion.21
  3.4 3.5 %select_reduce_fusion = (f32[16,2,16]{2,1,0:T(2,128)S(1)}, f32[16,2,16,512]{3,2,1,0:T(8,128)S(1)}) fusion(pred[16,512]{1,0:T(8,128)(4,1)S(1)} %iota_compare_fusion, bf16[16,2,16,128]{3,2,1,0:T(8,128)(2,1)S(1)} %bitcast.36, bf16[16,512,256]{2,1,0:T(8,128)(2,1)} %param.14), kind=kOutput, calls=%fused_computation.10 | convolution fusion | flops 67894784 | bytes 5384192 | tf_op jit(solution)/shard_map/sgjd,stgd->sgjt/dot_general | solution.py:268
  6.9 0.0 copy-start
  7.0 0.4 fusion.15
  7.4 0.0 copy-done.1
  7.4 2.0 %fusion.12 = f32[16,2,16,128]{3,2,1,0:T(8,128)S(1)} fusion(f32[16,2,16,512]{3,2,1,0:T(8,128)S(1)} %get-tuple-element.8, f32[16,2,16]{2,1,0:T(2,128)S(1)} %multiply_maximum_fusion, pred[16,512]{1,0:T(8,128)(4,1)S(1)} %iota_compare_fusion, f32[16,2,16]{2,1,0:T(2,128)S(1)} %get-tuple-element.5, f32[16,2,128]{2,1,0:T(2,128)S(1)} %reshape.52, ...), kind=kOutput, calls=%fused_computation.8 | convolution fusion | flops 403374080 | bytes 5535744 | tf_op jit(solution)/shard_map/sgjt,stgd->sgjd/dot_general | solution.py:287
  9.4 0.0 copy-done
  9.4 0.9 bitcast_add_fusion.stream_ref
  10.2 81.1 %shard_map.109 = bf16[16,4096]{1,0:T(8,128)(2,1)} custom-call(f32[16,4096]{1,0:T(8,128)} %bitcast_add_fusion.stream_ref, f32[1,4096]{1,0:T(1,128)} %bitcast.41, bf16[3328,4096]{1,0:T(8,128)(2,1)} %gate_hbm.1, bf16[3328,4096]{1,0:T(8,128)(2,1)} %up_hbm.1, bf16[3328,4096]{1,0:T(8,128)(2,1)} %down_hbm.1), custom_call_target="tpu_custom_call" | custom-call | tf_op jit(solution)/shard_map/pallas_call | solution.py:217
  91.3 1.6 %copy.38 = bf16[16,4096]{1,0:T(8,128)(2,1)} copy(bf16[16,4096]{1,0:T(8,128)(2,1)} %shard_map.109) | data formatting | bytes 262144
  (2 shorter events, 0.0 us)
Async XLA Ops:
  2.1 5.3 %copy-start.1 = (bf16[16,512,256]{2,1,0:T(8,128)(2,1)S(1)}, bf16[16,512,256]{2,1,0:T(8,128)(2,1)}, u32[]{:S(2)}) copy-start(bf16[16,512,256]{2,1,0:T(8,128)(2,1)} %param.15) | copy-start | bytes 12582916
  6.9 2.4 %copy-start = (bf16[16,4096]{1,0:T(8,128)(2,1)S(1)}, bf16[16,4096]{1,0:T(8,128)(2,1)}, u32[]{:S(2)}) copy-start(bf16[16,4096]{1,0:T(8,128)(2,1)} %param.17) | copy-start | bytes 393220

commit v2 on v1

--- a/solution.py
+++ b/solution.py
@@ -15,26 +15,25 @@
 
 
 highest = lax.Precision.HIGHEST
-contract_last = (((1,), (1,)), ((), ()))
 low_value = -1e30
 
 
 MESH = pl.DeviceIdType.MESH
-HIDDEN_LAG = 3
-DOWN_LAG = 6
+HIDDEN_LAG = 2
+DOWN_LAG = 4
 SLOT_BYTES = 40 * 2**20
 
 
 def block_kernel(
     sizes,
     stream_ref, gain_ref, gate_hbm, up_hbm, down_hbm, out_ref,
-    wbuf, ssum, xg, tf, pb, precv, hid, acc, psd, prv, zs, zr,
+    wbuf, ssum, xg, xt, tf, pb, precv, hid, acc, psd, prv, zs, zr,
     wsem, ss_send, ss_recv, ag_send, ag_recv, agp_send, agp_recv,
     rs_send, rs_recv, hg_send, hg_recv, pr_send, pr_recv, z_send, z_recv,
 ):
     reqs, heads, chunks, unit, slots, rows, feats, total_feats = sizes
     block = reqs * 2 * rows
-    part = block // heads
+    part = unit // heads
     my_req = lax.axis_index("req")
     my_head = lax.axis_index("head")
     my_pair = lax.axis_index("pair")
@@ -100,6 +99,8 @@
         pair_copy(owner, other).wait_recv()
 
     acc[...] = jnp.zeros_like(acc)
+    for c in range(0, feats, 512):
+        xt[c : c + 512, :] = xg[:, :, :, c : c + 512].reshape(block, 512).T
 
     def sum_copy(chunk, owner, peer):
         return remote(
@@ -117,10 +118,9 @@
             for side, hbm in enumerate((gate_hbm, up_hbm)):
                 slot = lax.rem(2 * t + side, slots)
                 load_of(hbm, t, slot).wait()
-                x = xg[...].reshape(block, feats)
-                sums = lax.dot_general(
-                    x, wbuf[slot], contract_last, preferred_element_type=jnp.float32
-                ).reshape(heads, part, unit)
+                sums = jnp.dot(
+                    wbuf[slot], xt[...], preferred_element_type=jnp.float32
+                ).reshape(heads, part, block)
                 tf[t, :, side] = sums
                 pb[t, :, side] = sums.astype(jnp.bfloat16)
             for peer in head_peers:
@@ -157,7 +157,7 @@
             load_of(down_hbm, k, slot).wait()
             for peer in head_peers:
                 hidden_copy(k, peer, peer).wait_recv()
-            h = hid[k].reshape(block, unit)
+            h = hid[k].reshape(unit, block).T
             tile = 512
             for c in range(0, feats, tile):
                 d = jnp.dot(h, wbuf[slot, :, c : c + tile], preferred_element_type=jnp.float32)
@@ -204,11 +204,11 @@
 def feed_forward(reqs, heads, stream, norm_gain, gate_weight, up_weight, down_weight):
     rows, feats = stream.shape
     units = gate_weight.shape[0]
-    unit = max(u for u in range(16, 257, 16) if units % u == 0)
+    unit = max(u for u in range(16 * heads, 257, 16 * heads) if units % u == 0)
     chunks = units // unit
     slots = min(3 * chunks, SLOT_BYTES // (unit * feats * 2) // 2 * 2)
     block = reqs * 2 * rows
-    part = block // heads
+    part = unit // heads
     sizes = (reqs, heads, chunks, unit, slots, rows, feats, D)
     bf16, f32 = jnp.bfloat16, jnp.float32
     dma = pltpu.SemaphoreType.DMA
@@ -223,10 +223,11 @@
             pltpu.VMEM((slots, unit, feats), bf16),
             pltpu.VMEM((heads, rows, HEAD_DIM), f32),
             pltpu.VMEM((reqs, 2, rows, feats), bf16),
-            pltpu.VMEM((chunks, heads, 2, part, unit), f32),
-            pltpu.VMEM((chunks, heads, 2, part, unit), bf16),
-            pltpu.VMEM((chunks, heads, 2, part, unit), bf16),
-            pltpu.VMEM((chunks, heads, part, unit), bf16),
+            pltpu.VMEM((feats, block), bf16),
+            pltpu.VMEM((chunks, heads, 2, part, block), f32),
+            pltpu.VMEM((chunks, heads, 2, part, block), bf16),
+            pltpu.VMEM((chunks, heads, 2, part, block), bf16),
+            pltpu.VMEM((chunks, heads, part, block), bf16),
             pltpu.VMEM((reqs, 2, rows, feats), f32),
             pltpu.VMEM((reqs, rows, feats), bf16),
             pltpu.VMEM((reqs, rows, feats), bf16),

time: 93.1 us -> 82.2 us (0.88)
  Pallas kernels: 81.1 us -> 70.1 us
    pallas_call x1, Pallas kernels: 81.1 us -> 70.1 us  [feed_forward(): pl.pallas_call(functools.partial(block_kernel, sizes), out_shape=jax.Shap...]
where the time goes in v2:
time: 82.2 us; the launch traced here: 81.9 us
  Pallas kernels  70.1 us (85%)
  matrix products  5.65 us (7%)
  local copies, waits for them, and re-layouts  4.08 us (5%)
  other arithmetic  2.01 us (2%)
    pallas_call x1, Pallas kernels, feed_forward(): pl.pallas_call(functools.partial(block_kernel, sizes), out_shape=jax.Shap...  70.1 us
    dot_general x1, matrix products, local(): jnp.einsum('sgjd,stgd->sgjt', query_heads, key_heads, preferred_element_t...  3.52 us
    unnamed x6, local copies, waits for them, and re-layouts  2.67 us
    dot_general x1, matrix products, local(): jnp.einsum('sgjt,stgd->sgjd', weights, value_heads, precision=highest)  1.95 us

profile of v2, /device:TPU:0, one launch (start us, length us, event | category | flops | bytes accessed | tf_op | source)
XLA Modules:
  0.0 81.9 jit_solution(11876698138568801942)
XLA Ops:
  0.0 0.7 iota_compare_fusion
  0.7 0.7 reshape.56
  1.4 0.7 reshape.52
  2.1 0.0 copy-start.1
  2.2 1.1 %copy.18 = bf16[2,8,32,128]{3,2,1,0:T(8,128)(2,1)S(1)} copy(bf16[2,8,32,128]{3,1,2,0:T(8,128)(2,1)} %bitcast.38) | data formatting | bytes 262144
  3.2 0.2 fusion.21
  3.4 3.5 %select_reduce_fusion = (f32[16,2,16]{2,1,0:T(2,128)S(1)}, f32[16,2,16,512]{3,2,1,0:T(8,128)S(1)}) fusion(pred[16,512]{1,0:T(8,128)(4,1)S(1)} %iota_compare_fusion, bf16[16,2,16,128]{3,2,1,0:T(8,128)(2,1)S(1)} %bitcast.36, bf16[16,512,256]{2,1,0:T(8,128)(2,1)} %param.14), kind=kOutput, calls=%fused_computation.10 | convolution fusion | flops 67894784 | bytes 5384192 | tf_op jit(solution)/shard_map/sgjd,stgd->sgjt/dot_general | solution.py:269
  6.9 0.0 copy-start
  7.0 0.4 fusion.15
  7.4 0.0 copy-done.1
  7.4 2.0 %fusion.12 = f32[16,2,16,128]{3,2,1,0:T(8,128)S(1)} fusion(f32[16,2,16,512]{3,2,1,0:T(8,128)S(1)} %get-tuple-element.8, f32[16,2,16]{2,1,0:T(2,128)S(1)} %multiply_maximum_fusion, pred[16,512]{1,0:T(8,128)(4,1)S(1)} %iota_compare_fusion, f32[16,2,16]{2,1,0:T(2,128)S(1)} %get-tuple-element.5, f32[16,2,128]{2,1,0:T(2,128)S(1)} %reshape.52, ...), kind=kOutput, calls=%fused_computation.8 | convolution fusion | flops 403374080 | bytes 5535744 | tf_op jit(solution)/shard_map/sgjt,stgd->sgjd/dot_general | solution.py:288
  9.4 0.0 copy-done
  9.4 0.9 %bitcast_add_fusion.stream_ref = f32[16,4096]{1,0:T(8,128)} fusion(f32[2,8,32,128]{3,2,1,0:T(8,128)S(1)} %bitcast.37, bf16[16,4096]{1,0:T(8,128)(2,1)S(1)} %copy-done), kind=kLoop, calls=%fused_computation.15 | loop fusion | flops 131072 | bytes 655360 | tf_op jit(solution)/shard_map/add | solution.py:293
  10.2 70.1 %shard_map.109 = bf16[16,4096]{1,0:T(8,128)(2,1)} custom-call(f32[16,4096]{1,0:T(8,128)} %bitcast_add_fusion.stream_ref, f32[1,4096]{1,0:T(1,128)} %bitcast.41, bf16[3328,4096]{1,0:T(8,128)(2,1)} %gate_hbm.1, bf16[3328,4096]{1,0:T(8,128)(2,1)} %up_hbm.1, bf16[3328,4096]{1,0:T(8,128)(2,1)} %down_hbm.1), custom_call_target="tpu_custom_call" | custom-call | tf_op jit(solution)/shard_map/pallas_call | solution.py:217
  80.4 1.6 %copy.38 = bf16[16,4096]{1,0:T(8,128)(2,1)} copy(bf16[16,4096]{1,0:T(8,128)(2,1)} %shard_map.109) | data formatting | bytes 262144
  (2 shorter events, 0.0 us)
Async XLA Ops:
  2.1 5.3 %copy-start.1 = (bf16[16,512,256]{2,1,0:T(8,128)(2,1)S(1)}, bf16[16,512,256]{2,1,0:T(8,128)(2,1)}, u32[]{:S(2)}) copy-start(bf16[16,512,256]{2,1,0:T(8,128)(2,1)} %param.15) | copy-start | bytes 12582916
  6.9 2.4 %copy-start = (bf16[16,4096]{1,0:T(8,128)(2,1)S(1)}, bf16[16,4096]{1,0:T(8,128)(2,1)}, u32[]{:S(2)}) copy-start(bf16[16,4096]{1,0:T(8,128)(2,1)} %param.17) | copy-start | bytes 393220

commit v3 on v2

--- a/solution.py
+++ b/solution.py
@@ -19,8 +19,8 @@
 
 
 MESH = pl.DeviceIdType.MESH
-HIDDEN_LAG = 2
-DOWN_LAG = 4
+HIDDEN_LAG = 1
+DOWN_LAG = 3
 SLOT_BYTES = 40 * 2**20
 
 

time: 82.2 us -> 89.9 us (1.094)
  Pallas kernels: 70.1 us -> 77.8 us
    pallas_call x1, Pallas kernels: 70.1 us -> 77.8 us  [feed_forward(): pl.pallas_call(functools.partial(block_kernel, sizes), out_shape=jax.Shap...]
where the time goes in v3:
time: 89.9 us; the launch traced here: 89.6 us
  Pallas kernels  77.8 us (87%)
  matrix products  5.65 us (6%)
  local copies, waits for them, and re-layouts  4.08 us (5%)
  other arithmetic  2.01 us (2%)
    pallas_call x1, Pallas kernels, feed_forward(): pl.pallas_call(functools.partial(block_kernel, sizes), out_shape=jax.Shap...  77.8 us
    dot_general x1, matrix products, local(): jnp.einsum('sgjd,stgd->sgjt', query_heads, key_heads, preferred_element_t...  3.52 us
    unnamed x6, local copies, waits for them, and re-layouts  2.67 us
    dot_general x1, matrix products, local(): jnp.einsum('sgjt,stgd->sgjd', weights, value_heads, precision=highest)  1.95 us

profile of v3, /device:TPU:0, one launch (start us, length us, event | category | flops | bytes accessed | tf_op | source)
XLA Modules:
  0.0 89.6 jit_solution(15569905472273307213)
XLA Ops:
  0.0 0.7 iota_compare_fusion
  0.7 0.7 reshape.56
  1.4 0.7 reshape.52
  2.1 0.0 copy-start.1
  2.2 1.1 %copy.18 = bf16[2,8,32,128]{3,2,1,0:T(8,128)(2,1)S(1)} copy(bf16[2,8,32,128]{3,1,2,0:T(8,128)(2,1)} %bitcast.38) | data formatting | bytes 262144
  3.2 0.2 fusion.21
  3.4 3.5 %select_reduce_fusion = (f32[16,2,16]{2,1,0:T(2,128)S(1)}, f32[16,2,16,512]{3,2,1,0:T(8,128)S(1)}) fusion(pred[16,512]{1,0:T(8,128)(4,1)S(1)} %iota_compare_fusion, bf16[16,2,16,128]{3,2,1,0:T(8,128)(2,1)S(1)} %bitcast.36, bf16[16,512,256]{2,1,0:T(8,128)(2,1)} %param.14), kind=kOutput, calls=%fused_computation.10 | convolution fusion | flops 67894784 | bytes 5384192 | tf_op jit(solution)/shard_map/sgjd,stgd->sgjt/dot_general | solution.py:269
  6.9 0.0 copy-start
  7.0 0.4 fusion.15
  7.4 0.0 copy-done.1
  7.4 2.0 %fusion.12 = f32[16,2,16,128]{3,2,1,0:T(8,128)S(1)} fusion(f32[16,2,16,512]{3,2,1,0:T(8,128)S(1)} %get-tuple-element.8, f32[16,2,16]{2,1,0:T(2,128)S(1)} %multiply_maximum_fusion, pred[16,512]{1,0:T(8,128)(4,1)S(1)} %iota_compare_fusion, f32[16,2,16]{2,1,0:T(2,128)S(1)} %get-tuple-element.5, f32[16,2,128]{2,1,0:T(2,128)S(1)} %reshape.52, ...), kind=kOutput, calls=%fused_computation.8 | convolution fusion | flops 403374080 | bytes 5535744 | tf_op jit(solution)/shard_map/sgjt,stgd->sgjd/dot_general | solution.py:288
  9.4 0.0 copy-done
  9.4 0.9 bitcast_add_fusion.stream_ref
  10.2 77.8 %shard_map.109 = bf16[16,4096]{1,0:T(8,128)(2,1)} custom-call(f32[16,4096]{1,0:T(8,128)} %bitcast_add_fusion.stream_ref, f32[1,4096]{1,0:T(1,128)} %bitcast.41, bf16[3328,4096]{1,0:T(8,128)(2,1)} %gate_hbm.1, bf16[3328,4096]{1,0:T(8,128)(2,1)} %up_hbm.1, bf16[3328,4096]{1,0:T(8,128)(2,1)} %down_hbm.1), custom_call_target="tpu_custom_call" | custom-call | tf_op jit(solution)/shard_map/pallas_call | solution.py:217
  88.1 1.6 %copy.38 = bf16[16,4096]{1,0:T(8,128)(2,1)} copy(bf16[16,4096]{1,0:T(8,128)(2,1)} %shard_map.109) | data formatting | bytes 262144
  (2 shorter events, 0.0 us)
Async XLA Ops:
  2.1 5.3 %copy-start.1 = (bf16[16,512,256]{2,1,0:T(8,128)(2,1)S(1)}, bf16[16,512,256]{2,1,0:T(8,128)(2,1)}, u32[]{:S(2)}) copy-start(bf16[16,512,256]{2,1,0:T(8,128)(2,1)} %param.15) | copy-start | bytes 12582916
  6.9 2.4 %copy-start = (bf16[16,4096]{1,0:T(8,128)(2,1)S(1)}, bf16[16,4096]{1,0:T(8,128)(2,1)}, u32[]{:S(2)}) copy-start(bf16[16,4096]{1,0:T(8,128)(2,1)} %param.17) | copy-start | bytes 393220
